TPU v7x, 32 devices: a whole 2x2x4 slice. The times are simulated.
32 devices in a mesh: mem: 4 (over y, x), cell: 8 (over z, core).
Axes of the slice: x: 2, y: 2, z: 4, core: 2. Of those that a mesh axis runs over, the one named last changes fastest.
Arguments:
- depth: float32 [64, 131072], P('mem', 'cell'), may hold values from 1 to 3
- discharge: float32 [64, 131072], P('mem', 'cell'), may hold values from -1.5 to 1.5
- gate: int32 [131072], P('cell'), may hold values from 0 to 1, as said below
- pump: int32 [2, 131072], P(None, 'cell'), may hold values 0 or 1
- pump_rate: float32 [131072], P('cell'), may hold values from 1 to 5
- obs_index: int32 [8, 512], P('cell'), may hold values from 0 to 16383, as said below
- obs_value: float32 [8, 512], P('cell'), may hold values from 1 to 3
- obs_error: float32 [8, 512], P('cell'), may hold values from 0.25 to 1.04
Outputs:
- depth_analysis: float32 [64, 131072], P('mem', 'cell')
- discharge_analysis: float32 [64, 131072], P('mem', 'cell')
Inputs may be any that keep to these rules, and one draw needn't show every extreme that they name: The gate on the first face of every slab after the first (cells s * 16384 with s >= 1) is open. `obs_index`: the offsets of one slab are distinct.
All inputs are finite; a program needn't handle non-finite values. No bound on the sum of `pump` on one device may be relied on, other than what follows from the above.
Results may differ from a plain program's by a relative error of at most 0.0003.
Values sent between devices are 32-bit elements; how exact they have to be, the bound alone decides.
A program may use at most 64 MiB of HBM per device.

v0:
```python
import jax
import jax.numpy as jnp
from jax import lax
from jax.sharding import PartitionSpec as P

PER = 512
NS_ITERS = 12


gravity = 9.81
step_dt = 0.06


def padded_2(block, sides, width):
    for axis, dim in sides:
        count = lax.axis_size(axis)
        forward = [(i, i + 1) for i in range(count - 1)]
        backward = [(target, source) for source, target in forward]
        low = lax.ppermute(
            lax.slice_in_dim(block, block.shape[dim] - width, None, axis=dim), axis, forward
        )
        high = lax.ppermute(lax.slice_in_dim(block, 0, width, axis=dim), axis, backward)
        block = jnp.concatenate([low, block, high], axis=dim)
    return block


def face_fluxes(depth_left, flow_left, depth_right, flow_right, faces):
    opened = faces > 0.5
    safe_dl = jnp.where(opened, depth_left, 1.0)
    safe_fl = jnp.where(opened, flow_left, 0.0)
    safe_dr = jnp.where(opened, depth_right, 1.0)
    safe_fr = jnp.where(opened, flow_right, 0.0)
    speed_left = safe_fl / safe_dl
    speed_right = safe_fr / safe_dr
    wave_left = jnp.sqrt(gravity * safe_dl)
    wave_right = jnp.sqrt(gravity * safe_dr)
    slowest = jnp.minimum(jnp.minimum(speed_left - wave_left, speed_right - wave_right), 0.0)
    fastest = jnp.maximum(jnp.maximum(speed_left + wave_left, speed_right + wave_right), 0.0)
    moment_left = safe_fl * speed_left + 0.5 * gravity * safe_dl * safe_dl
    moment_right = safe_fr * speed_right + 0.5 * gravity * safe_dr * safe_dr
    spread = fastest - slowest
    mass = (
        fastest * safe_fl - slowest * safe_fr + slowest * fastest * (safe_dr - safe_dl)
    ) / spread
    moment = (
        fastest * moment_left - slowest * moment_right + slowest * fastest * (safe_fr - safe_fl)
    ) / spread
    mass = jnp.where(opened, mass, 0.0)
    left_side = jnp.where(opened, moment, 0.5 * gravity * depth_left * depth_left)
    right_side = jnp.where(opened, moment, 0.5 * gravity * depth_right * depth_right)
    return (mass, left_side, right_side)


def advance(depth_pad, flow_pad, faces, inflow):
    mass, left_side, right_side = face_fluxes(
        depth_pad[..., :-1], flow_pad[..., :-1], depth_pad[..., 1:], flow_pad[..., 1:], faces
    )
    depth_new = depth_pad[..., 1:-1] - step_dt * (mass[..., 1:] - mass[..., :-1]) + step_dt * inflow
    flow_new = flow_pad[..., 1:-1] - step_dt * (left_side[..., 1:] - right_side[..., :-1])
    return (depth_new, flow_new)


def batch_product(first, second):
    return jnp.einsum("uij,ujk->uik", first, second, precision=lax.Precision.HIGHEST)


def transform_units(grams, cross, factor_rho):
    count = grams.shape[-1]
    identity = jnp.eye(count, dtype=jnp.float32)
    system = identity + factor_rho * factor_rho / (count - 1) * grams
    norm_scale = jnp.sqrt(jnp.sum(system * system, axis=(1, 2)))
    iterate = system / norm_scale[:, None, None]
    inverse = jnp.broadcast_to(identity, system.shape)

    def newton_step(turn, carry):
        current, invroot = carry
        factor = 1.5 * identity - 0.5 * batch_product(invroot, current)
        return (batch_product(current, factor), batch_product(factor, invroot))

    iterate, inverse = lax.fori_loop(0, NS_ITERS, newton_step, (iterate, inverse))
    root_weight = inverse / jnp.sqrt(norm_scale)[:, None, None]
    solved = batch_product(inverse, inverse) / norm_scale[:, None, None]
    mean_weight = (
        factor_rho
        / (count - 1)
        * jnp.einsum("uij,uj->ui", solved, cross, precision=lax.Precision.HIGHEST)
    )
    return factor_rho * (root_weight + mean_weight[:, :, None])


def window_sums(block_grams, block_cross):
    grams = block_grams[:-2] + block_grams[1:-1] + block_grams[2:]
    cross = block_cross[:-2] + block_cross[1:-1] + block_cross[2:]
    return (grams, cross)


def shards(depth, discharge, gate, pump, pump_rate, obs_index, obs_value, obs_error):
    member_rows = depth.shape[0]
    cell_count = depth.shape[1]
    slab_count = lax.axis_size("cell")
    quarter_count = lax.axis_size("mem")
    members = member_rows * quarter_count
    quart_cells = cell_count // quarter_count
    sub_count = quart_cells // PER
    obs_count = obs_index.shape[1]
    total_obs = obs_count * slab_count
    slab_here = lax.axis_index("cell")
    first_slab = slab_here == 0
    last_slab = slab_here == slab_count - 1
    left_open = gate.at[0].set(jnp.where(first_slab, 0, gate[0]))
    right_face = jnp.where(last_slab, 0, 1).astype(jnp.int32).reshape(1)
    faces = jnp.concatenate([left_open, right_face]).astype(jnp.float32)
    depth_now, flow_now = (depth, discharge)
    for step in range(pump.shape[0]):
        padded = padded_2(jnp.stack([depth_now, flow_now]), (("cell", 2),), 1)
        inflow = pump_rate * pump[step].astype(jnp.float32)
        depth_now, flow_now = advance(padded[0], padded[1], faces, inflow)
    offsets = obs_index[0]
    precision_obs = 1.0 / obs_error[0]
    values_obs = obs_value[0]
    value_row = jnp.zeros((cell_count,), jnp.float32).at[offsets].set(values_obs)
    prec_row = jnp.zeros((cell_count,), jnp.float32).at[offsets].set(precision_obs)
    stacked = jnp.concatenate([depth_now, value_row[None, :], prec_row[None, :]], axis=0)
    extended = padded_2(stacked, (("cell", 1),), PER)
    row_total = extended.shape[0]
    seen_local = depth_now[:, offsets]
    seen_all = lax.all_gather(seen_local, "mem", axis=0, tiled=True)
    seen_mean = jnp.mean(seen_all, axis=0)
    scaled_seen = (seen_all - seen_mean[None, :]) * precision_obs[None, :]
    innov_seen = (values_obs - seen_mean) * precision_obs
    total_misfit, total_spread = lax.psum(
        (jnp.sum(innov_seen * innov_seen), jnp.sum(scaled_seen * scaled_seen) / (members - 1)),
        "cell",
    )
    head = extended[:, :cell_count].reshape(row_total, quarter_count, quart_cells)[:, :, :PER]
    core = extended[:, PER : PER + cell_count].reshape(row_total, quarter_count, quart_cells)
    tail = extended[:, 2 * PER :].reshape(row_total, quarter_count, quart_cells)[
        :, :, quart_cells - PER :
    ]
    windows = jnp.concatenate([head, core, tail], axis=2)
    flow_quarters = flow_now.reshape(member_rows, quarter_count, quart_cells)
    moved_depth, moved_flow = (
        lax.all_to_all(windows[:member_rows], "mem", split_axis=1, concat_axis=0, tiled=True),
        lax.all_to_all(flow_quarters, "mem", split_axis=1, concat_axis=0, tiled=True),
    )
    window_depth = moved_depth[:, 0]
    quarter_flow = moved_flow[:, 0]
    obs_window = lax.dynamic_index_in_dim(
        windows[member_rows:], lax.axis_index("mem"), 1, keepdims=False
    )
    window_mean = jnp.mean(window_depth, axis=0)
    scaled = (window_depth - window_mean[None, :]) * obs_window[1][None, :]
    innov = (obs_window[0] - window_mean) * obs_window[1]
    blocks = scaled.reshape(members, sub_count + 2, PER)
    block_grams = jnp.einsum("ibr,jbr->bij", blocks, blocks, precision=lax.Precision.HIGHEST)
    block_cross = jnp.einsum(
        "ibr,br->bi", blocks, innov.reshape(sub_count + 2, PER), precision=lax.Precision.HIGHEST
    )
    grams, cross = window_sums(block_grams, block_cross)
    factor_rho = jnp.sqrt(total_misfit / (total_spread + total_obs))
    mixing = transform_units(grams, cross, factor_rho)
    fields = jnp.stack([window_depth[:, PER : PER + quart_cells], quarter_flow]).reshape(
        2, members, sub_count, PER
    )
    field_mean = jnp.mean(fields, axis=1, keepdims=True)
    analysed = field_mean + jnp.einsum(
        "fipr,pij->fjpr", fields - field_mean, mixing, precision=lax.Precision.HIGHEST
    )
    restored = lax.all_to_all(
        analysed.reshape(2, members, quart_cells), "mem", split_axis=1, concat_axis=2, tiled=True
    )
    return (restored[0], restored[1])


def solution(mesh):
    return jax.shard_map(
        shards,
        mesh=mesh,
        in_specs=(
            P("mem", "cell"),
            P("mem", "cell"),
            P("cell"),
            P(None, "cell"),
            P("cell"),
            P("cell", None),
            P("cell", None),
            P("cell", None),
        ),
        out_specs=(P("mem", "cell"), P("mem", "cell")),
        check_vma=False,
    )
```

profile of v0, /device:TPU:0, one launch (start us, length us, event | category | flops | bytes accessed | tf_op | source)
XLA Modules:
  0.0 180.7 jit_solution(2937933916349297083)
XLA Ops:
  3.7 3.0 %collective-permute-start = (f32[2,16,1]{2,1,0:T(8,128)S(1)}, f32[2,16,1]{2,1,0:T(8,128)S(1)}, u32[]{:S(2)}, u32[]{:S(2)}) collective-permute-start(f32[2,16,1]{2,1,0:T(8,128)S(1)} %get-tuple-element.88), channel_id=1, source_target_pairs={{0,1},{1,2},{2,3},{3,4},{4,5},{5,6},{6,7},{8,9},{9,10},{10,11},{11... | collective-permute-start | bytes 392 | tf_op jit(solution)/shard_map/ppermute | solution.py:19
  10.4 2.5 %scatter_custom_fusion.1 = f32[16384]{0:T(1024)S(1)} fusion(s32[512]{0:T(512)S(1)} %bitcast.152, f32[512]{0:T(512)S(1)} %bitcast.146, f32[]{:T(128)} %constant.71.clone.1), kind=kCustom, calls=%fused_computation.138 | custom fusion | bytes 65540 | tf_op jit(solution)/shard_map/scatter | solution.py:122
  12.9 2.5 %scatter_custom_fusion = f32[16384]{0:T(1024)S(1)} fusion(s32[512]{0:T(512)S(1)} %bitcast.153, f32[512]{0:T(512)S(1)} %bitcast.154, f32[]{:T(128)} %constant.71.clone.1), kind=kCustom, calls=%fused_computation.140 | custom fusion | bytes 65540 | tf_op jit(solution)/shard_map/scatter | solution.py:121
  15.4 3.1 %concatenate.34 = f32[2,16,16386]{2,1,0:T(8,128)S(1)} concatenate(f32[2,16,1]{2,1,0:T(8,128)S(1)} %collective-permute-done, f32[2,16,16384]{2,1,0:T(8,128)} %pad_maximum_fusion, f32[2,16,1]{2,1,0:T(8,128)S(1)} %collective-permute-done.1), dimensions={2} | concatenate | bytes 4194816 | tf_op jit(solution)/shard_map/concatenate | solution.py:23
  18.6 2.2 %fusion.12 = (f32[16,16385]{1,0:T(8,128)S(1)}, f32[16,16385]{1,0:T(8,128)S(1)}, f32[16,16385]{1,0:T(8,128)S(1)}, f32[16,16385]{1,0:T(8,128)S(1)}) fusion(f32[16,16386]{1,0:T(8,128)S(1)} %get-tuple-element.82, pred[16385]{0:T(1024)(128)(4,1)S(1)} %fusion.58, f32[16,16386]{1,0:T(8,128)S(1)} %get-tuple-element.81), kind=kLoop, calls=%fused_computation.43 | loop fusion | flops 10748560 | bytes 8405505 | tf_op jit(solution)/shard_map/div | solution.py:45
  23.6 5.2 %collective-permute-start.2 = (f32[2,16,1]{2,1,0:T(8,128)S(1)}, f32[2,16,1]{2,1,0:T(8,128)S(1)}, u32[]{:S(2)}, u32[]{:S(2)}) collective-permute-start(f32[2,16,1]{2,1,0:T(8,128)S(1)} %get-tuple-element.86), channel_id=1, source_target_pairs={{0,1},{1,2},{2,3},{3,4},{4,5},{5,6},{6,7},{8,9},{9,10},{10,11},{11... | collective-permute-start | bytes 392 | tf_op jit(solution)/shard_map/ppermute | solution.py:19
  30.3 3.1 %concatenate.36 = f32[2,16,16386]{2,1,0:T(8,128)S(1)} concatenate(f32[2,16,1]{2,1,0:T(8,128)S(1)} %collective-permute-done.2, f32[2,16,16384]{2,1,0:T(8,128)} %pad_maximum_fusion.1, f32[2,16,1]{2,1,0:T(8,128)S(1)} %collective-permute-done.3), dimensions={2} | concatenate | bytes 4194816 | tf_op jit(solution)/shard_map/concatenate | solution.py:23
  33.5 2.2 %fusion.19 = (f32[16,16385]{1,0:T(8,128)S(1)}, f32[16,16385]{1,0:T(8,128)S(1)}, f32[16,16385]{1,0:T(8,128)S(1)}, f32[16,16385]{1,0:T(8,128)S(1)}) fusion(f32[16,16386]{1,0:T(8,128)S(1)} %get-tuple-element.80, pred[16385]{0:T(1024)(128)(4,1)S(1)} %fusion.58, f32[16,16386]{1,0:T(8,128)S(1)} %get-tuple-element.79), kind=kLoop, calls=%fused_computation.50 | loop fusion | flops 10748560 | bytes 8405505 | tf_op jit(solution)/shard_map/div | solution.py:45
  36.3 3.6 %collective-permute-start.4 = (f32[18,512]{1,0:T(8,128)S(1)}, f32[18,512]{1,0:T(8,128)S(1)}, u32[]{:S(2)}, u32[]{:S(2)}) collective-permute-start(f32[18,512]{1,0:T(8,128)S(1)} %get-tuple-element.91), channel_id=1, source_target_pairs={{0,1},{1,2},{2,3},{3,4},{4,5},{5,6},{6,7},{8,9},{9,10},{10,11},{11... | collective-permute-start | bytes 110600 | tf_op jit(solution)/shard_map/ppermute | solution.py:19
  42.2 4.6 %copy.124 = f32[16,16384]{0,1:T(8,128)} copy(f32[16,16384]{1,0:T(8,128)S(1)} %fusion.35) | data formatting | bytes 2097152 | tf_op jit(solution)/shard_map/add | solution.py:58
  47.8 4.5 %all-to-all-start.1 = ((f32[16,4,4096]{2,0,1:T(8,128)}), f32[16,4,4096]{2,0,1:T(8,128)}, u32[]{:S(2)}, u32[]{:S(2)}) async-start(f32[16,4,4096]{2,0,1:T(8,128)} %bitcast.97), calls=%async_computation.1 | async-start | bytes 2097152 | tf_op jit(solution)/shard_map/all_to_all | solution.py:144
  52.4 4.4 %gather_fusion = f32[512,16]{1,0:T(8,128)S(1)} fusion(f32[16,16384]{0,1:T(8,128)} %copy.124, s32[1024]{0:T(1024)S(1)} %pad_clamp_fusion), kind=kCustom, calls=%fused_computation | custom fusion | bytes 67584 | tf_op jit(solution)/shard_map/gather | solution.py:126
  56.9 12.8 %all-gather = f32[64,512]{1,0:T(8,128)S(1)} all-gather(f32[16,512]{1,0:T(8,128)S(1)} %copy.125), channel_id=2, replica_groups=mesh['mem'=4,'cell'=8] {'mem'}, dimensions={0}, use_global_device_ids=true | all-gather | bytes 163840 | tf_op jit(solution)/shard_map/all_gather | solution.py:127
  71.6 3.1 %reshape.149 = f32[18,4,4096]{2,1,0:T(4,128)} reshape(f32[18,16384]{1,0:T(8,128)} %get-tuple-element.89) | data formatting | bytes 2359296 | tf_op jit(solution)/shard_map/reshape | solution.py:135
  79.9 3.7 %all-to-all-start = ((f32[16,4,5120]{2,0,1:T(8,128)}), f32[16,4,5120]{2,0,1:T(8,128)S(1)}, u32[]{:S(2)}, u32[]{:S(2)}) async-start(f32[16,4,5120]{2,0,1:T(8,128)} %slice.254), calls=%async_computation | async-start | bytes 2621440 | tf_op jit(solution)/shard_map/all_to_all | solution.py:143
  85.4 16.1 %all-reduce = (f32[]{:T(128)}, f32[]{:T(128)}) all-reduce(f32[]{:T(128)} %get-tuple-element.104, f32[]{:T(128)S(6)} %div.103), channel_id=1, replica_groups=mesh['mem'=4,'cell'=8] {'cell'}, use_global_device_ids=true, to_apply=%region_5.6 | all-reduce | flops 2 | bytes 16 | tf_op jit(solution)/shard_map/psum | solution.py:131
  103.5 2.8 %copy.150 = f32[8,8,8,512]{3,2,1,0:T(8,128)} copy(f32[8,8,8,512]{3,1,2,0:T(8,128)} %bitcast.55) | data formatting | bytes 2097152
  111.0 1.9 %subtract_multiply_fusion = f32[64,10,512]{2,1,0:T(8,128)S(1)} fusion(f32[64,10,512]{2,1,0:T(8,128)} %squeeze.49, f32[10,512]{1,0:T(8,128)S(1)} %mul.260, f32[10,512]{1,0:T(8,128)S(1)} %div.108), kind=kLoop, calls=%fused_computation.22 | loop fusion | flops 655360 | bytes 2662400 | tf_op jit(solution)/shard_map/mul | solution.py:152
  112.9 2.8 %fusion.43 = f32[10,64,64]{2,1,0:T(8,128)S(1)} fusion(f32[64,10,512]{2,1,0:T(8,128)S(1)} %subtract_multiply_fusion), kind=kOutput, calls=%fused_computation.98 | convolution fusion | flops 251658240 | bytes 1474560 | tf_op jit(solution)/shard_map/ibr,jbr->bij/dot_general | solution.py:155
  115.7 2.0 %fusion.41 = f32[10,1,64]{2,1,0:T(1,128)S(1)} fusion(f32[64,10,512]{2,1,0:T(8,128)S(1)} %subtract_multiply_fusion, f32[10,512,1]{1,0,2:T(8,128)S(1)} %multiply_bitcast_fusion), kind=kOutput, calls=%fused_computation.96 | convolution fusion | flops 3932160 | bytes 1333760 | tf_op jit(solution)/shard_map/ibr,br->bi/dot_general | solution.py:156
  118.1 19.9 %while.14 = (s32[]{:T(128)}, f32[8,64,64]{1,2,0:T(8,128)S(1)}, f32[8,64,64]{2,1,0:T(8,128)S(1)}, s32[]{:T(128)}) while((s32[]{:T(128)}, f32[8,64,64]{1,2,0:T(8,128)S(1)}, f32[8,64,64]{2,1,0:T(8,128)S(1)}, s32[]{:T(128)}) %tuple.56), condition=%wide.region_11.12_spmd.clone, body=%wide.region_10.11_spmd.clone.sunk | while | flops 75571200 | bytes 1736757 | solution.py:80
  138.9 2.1 %bitcast_add_fusion = f32[2,64,8,512]{3,1,0,2:T(8,128)S(1)} fusion(f32[2,64,8,512]{3,1,0,2:T(8,128)S(1)} %copy_dynamic-update-slice_fusion, f32[2,8,512]{2,0,1:T(2,128)S(1)} %broadcast_multiply_fusion, f32[8,64,64]{2,1,0:T(8,128)S(1)} %get-tuple-element.36, f32[8,64]{1,0:T(8,128)S(1)} %broadcast_multiply_fusion.2, f32[8]{0:T(128)S(1)} %get-tuple-element.105, ...), kind=kOutput, calls=%fused_computation.19 | convolution fusion | flops 403800064 | bytes 4360228 | tf_op jit(solution)/shard_map/fipr,pij->fjpr/dot_general | solution.py:166
  142.3 2.8 %reshape.183 = f32[2,64,4096]{2,0,1:T(2,128)} reshape(f32[2,64,8,512]{3,2,0,1:T(8,128)S(1)} %copy.145) | data formatting | bytes 4194304 | tf_op jit(solution)/shard_map/reshape | solution.py:170
  145.1 29.7 %all_to_all.45 = f32[2,64,4096]{2,0,1:T(2,128)S(1)} all-to-all(f32[2,64,4096]{2,0,1:T(2,128)} %reshape.183), channel_id=1, replica_groups=mesh['mem'=4,'cell'=8] {'mem'}, dimensions={1} | all-to-all | bytes 4194304 | tf_op jit(solution)/shard_map/all_to_all | solution.py:169
  (180 shorter events, 55.6 us)
Async XLA Ops:
  1.5 5.9 %copy-start.2 = (f32[16,16384]{1,0:T(8,128)S(1)}, f32[16,16384]{1,0:T(8,128)}, u32[]{:S(2)}) copy-start(f32[16,16384]{1,0:T(8,128)} %param.12) | copy-start | bytes 3145732
  1.5 5.9 %copy-start.3 = (f32[16,16384]{1,0:T(8,128)S(1)}, f32[16,16384]{1,0:T(8,128)}, u32[]{:S(2)}) copy-start(f32[16,16384]{1,0:T(8,128)} %param.13) | copy-start | bytes 3145732
  2.5 13.0 %collective-permute-start.1 = (f32[2,16,1]{2,1,0:T(8,128)S(1)}, f32[2,16,1]{2,1,0:T(8,128)S(1)}, u32[]{:S(2)}, u32[]{:S(2)}) collective-permute-start(f32[2,16,1]{2,1,0:T(8,128)S(1)} %get-tuple-element.87), channel_id=1, source_target_pairs={{1,0},{2,1},{3,2},{4,3},{5,4},{6,5},{7,6},{9,8},{10,9},{11,10},{12... | collective-permute-start | bytes 392 | tf_op jit(solution)/shard_map/ppermute | solution.py:22
  3.7 11.7 %collective-permute-start = (f32[2,16,1]{2,1,0:T(8,128)S(1)}, f32[2,16,1]{2,1,0:T(8,128)S(1)}, u32[]{:S(2)}, u32[]{:S(2)}) collective-permute-start(f32[2,16,1]{2,1,0:T(8,128)S(1)} %get-tuple-element.88), channel_id=1, source_target_pairs={{0,1},{1,2},{2,3},{3,4},{4,5},{5,6},{6,7},{8,9},{9,10},{10,11},{11... | collective-permute-start | bytes 392 | tf_op jit(solution)/shard_map/ppermute | solution.py:19
  7.4 1.5 copy-start.13
  7.4 1.5 copy-start.14
  7.4 2.8 %copy-start.9 = (s32[2,16384]{1,0:T(2,128)S(1)}, s32[2,16384]{1,0:T(2,128)}, u32[]{:S(2)}) copy-start(s32[2,16384]{1,0:T(2,128)} %param.15) | copy-start | bytes 393220
  7.4 5.4 %copy-start.11 = (f32[16384]{0:T(1024)S(1)}, f32[16384]{0:T(1024)}, u32[]{:S(2)}) copy-start(f32[16384]{0:T(1024)} %param.16) | copy-start | bytes 196612
  7.4 5.5 %copy-start.12 = (f32[1,512]{1,0:T(1,128)S(1)}, f32[1,512]{1,0:T(1,128)}, u32[]{:S(2)}) copy-start(f32[1,512]{1,0:T(1,128)} %param.18) | copy-start | bytes 6148
  22.3 8.0 %collective-permute-start.3 = (f32[2,16,1]{2,1,0:T(8,128)S(1)}, f32[2,16,1]{2,1,0:T(8,128)S(1)}, u32[]{:S(2)}, u32[]{:S(2)}) collective-permute-start(f32[2,16,1]{2,1,0:T(8,128)S(1)} %get-tuple-element.85), channel_id=1, source_target_pairs={{1,0},{2,1},{3,2},{4,3},{5,4},{6,5},{7,6},{9,8},{10,9},{11,10},{12... | collective-permute-start | bytes 392 | tf_op jit(solution)/shard_map/ppermute | solution.py:22
  23.6 6.7 %collective-permute-start.2 = (f32[2,16,1]{2,1,0:T(8,128)S(1)}, f32[2,16,1]{2,1,0:T(8,128)S(1)}, u32[]{:S(2)}, u32[]{:S(2)}) collective-permute-start(f32[2,16,1]{2,1,0:T(8,128)S(1)} %get-tuple-element.86), channel_id=1, source_target_pairs={{0,1},{1,2},{2,3},{3,4},{4,5},{5,6},{6,7},{8,9},{9,10},{10,11},{11... | collective-permute-start | bytes 392 | tf_op jit(solution)/shard_map/ppermute | solution.py:19
  36.3 33.4 %collective-permute-start.4 = (f32[18,512]{1,0:T(8,128)S(1)}, f32[18,512]{1,0:T(8,128)S(1)}, u32[]{:S(2)}, u32[]{:S(2)}) collective-permute-start(f32[18,512]{1,0:T(8,128)S(1)} %get-tuple-element.91), channel_id=1, source_target_pairs={{0,1},{1,2},{2,3},{3,4},{4,5},{5,6},{6,7},{8,9},{9,10},{10,11},{11... | collective-permute-start | bytes 110600 | tf_op jit(solution)/shard_map/ppermute | solution.py:19
  40.0 29.8 %collective-permute-start.5 = (f32[18,512]{1,0:T(8,128)S(1)}, f32[18,512]{1,0:T(8,128)S(1)}, u32[]{:S(2)}, u32[]{:S(2)}) collective-permute-start(f32[18,512]{1,0:T(8,128)S(1)} %get-tuple-element.92), channel_id=1, source_target_pairs={{1,0},{2,1},{3,2},{4,3},{5,4},{6,5},{7,6},{9,8},{10,9},{11,10},{12... | collective-permute-start | bytes 110600 | tf_op jit(solution)/shard_map/ppermute | solution.py:22
  47.8 32.1 %all-to-all-start.1 = ((f32[16,4,4096]{2,0,1:T(8,128)}), f32[16,4,4096]{2,0,1:T(8,128)}, u32[]{:S(2)}, u32[]{:S(2)}) async-start(f32[16,4,4096]{2,0,1:T(8,128)} %bitcast.97), calls=%async_computation.1 | async-start | bytes 2097152 | tf_op jit(solution)/shard_map/all_to_all | solution.py:144
  69.7 1.9 %copy-start.6 = (f32[64,512]{1,0:T(8,128)}, f32[64,512]{1,0:T(8,128)S(1)}, u32[]{:S(2)}) copy-start(f32[64,512]{1,0:T(8,128)S(1)} %all-gather) | copy-start | bytes 393220
  71.6 4.1 %copy-start = (f32[18,16384]{1,0:T(8,128)S(1)}, f32[18,16384]{1,0:T(8,128)}, u32[]{:S(2)}) copy-start(f32[18,16384]{1,0:T(8,128)} %get-tuple-element.90) | copy-start | bytes 3538948
  75.7 2.8 %copy-start.4 = (f32[18,4,512]{2,0,1:T(8,128)}, f32[18,4,512]{2,0,1:T(8,128)S(1)}, u32[]{:S(2)}) copy-start(f32[18,4,512]{2,0,1:T(8,128)S(1)} %copy.119) | copy-start | bytes 442372
  79.9 4.3 %copy-start.7 = (f32[64,512]{1,0:T(8,128)S(1)}, f32[64,512]{1,0:T(8,128)}, u32[]{:S(2)}) copy-start(f32[64,512]{1,0:T(8,128)} %copy-done.6) | copy-start | bytes 393220
  79.9 22.8 %copy-start.5 = (f32[18,4,512]{2,0,1:T(8,128)S(1)}, f32[18,4,512]{2,0,1:T(8,128)}, u32[]{:S(2)}) copy-start(f32[18,4,512]{2,0,1:T(8,128)} %copy-done.4) | copy-start | bytes 442372
  79.9 26.4 %all-to-all-start = ((f32[16,4,5120]{2,0,1:T(8,128)}), f32[16,4,5120]{2,0,1:T(8,128)S(1)}, u32[]{:S(2)}, u32[]{:S(2)}) async-start(f32[16,4,5120]{2,0,1:T(8,128)} %slice.254), calls=%async_computation | async-start | bytes 2621440 | tf_op jit(solution)/shard_map/all_to_all | solution.py:143
  107.2 1.2 copy-start.1
  109.3 1.7 copy-start.10
  115.7 2.0 %copy-start.8 = (f32[64,64]{1,0:T(8,128)S(1)}, f32[64,64]{1,0:T(8,128)}, u32[]{:S(2)}) copy-start(f32[64,64]{1,0:T(8,128)} %fusion.67) | copy-start | bytes 49156
where the time goes:
time: 182 us; the launch traced here: 181 us
  blocking collectives  58.6 us (32%)
  local copies, waits for them, and re-layouts  49.4 us (27%)
  matrix products  26.1 us (14%)
  starting transfers between devices  23.9 us (13%)
  other arithmetic  18 us (10%)
  between operations  3.7 us (2%)
    all_to_all x1, blocking collectives, shards(): lax.all_to_all(analysed.reshape(2, members, quart_cells), 'mem', split_ax...  29.7 us
    dot_general x37, matrix products, batch_product(): jnp.einsum('uij,ujk->uik', first, second, precision=lax.Precision.HIGHEST)  18.8 us
    psum x1, blocking collectives, shards(): lax.psum((jnp.sum(innov_seen * innov_seen), jnp.sum(scaled_seen * scaled_...  16.1 us
    all_gather x1, blocking collectives, shards(): seen_all = lax.all_gather(seen_local, 'mem', axis=0, tiled=True)  12.8 us
    ppermute x3, starting transfers between devices, padded_2(): lax.ppermute(lax.slice_in_dim(block, block.shape[dim] - width, None, axis...  11.9 us
    unnamed x37, local copies, waits for them, and re-layouts  8.82 us
    concatenate x2, local copies, waits for them, and re-layouts, padded_2(): block = jnp.concatenate([low, block, high], axis=dim)  6.12 us
    another operation x5, other arithmetic, shards(): padded = padded_2(jnp.stack([depth_now, flow_now]), (('cell', 2),), 1)  5.41 us
  transfers between devices with their start and end apart: 8, of which 0 were waited for; matrix products, arithmetic and copies ran while one was open for 20% of the time, Pallas kernels for 0%

commit v1 on v0

v1 whole, which is shorter than its diff:
```python
import functools

import jax
import jax.numpy as jnp
from jax import lax
from jax.experimental import pallas as pl
from jax.experimental.pallas import tpu as pltpu
from jax.sharding import PartitionSpec as P

PER = 512
NS_ITERS = 12
LANES = 128
CHUNK = 1024
GROUP = 4
MESH = pl.DeviceIdType.MESH

gravity = 9.81
step_dt = 0.06


def rolled(x, shift):
    return pltpu.roll(x, shift % x.shape[1], 1)


def advance(h, q, opened, inflow):
    u = q / h
    c = jnp.sqrt(gravity * h)
    low = u - c
    top = u + c
    still = (0.5 * gravity) * h * h
    moment = q * u + still
    h_left = rolled(h, 1)
    q_left = rolled(q, 1)
    still_left = rolled(still, 1)
    moment_left = rolled(moment, 1)
    a = jnp.minimum(jnp.minimum(rolled(low, 1), low), 0.0)
    b = jnp.maximum(jnp.maximum(rolled(top, 1), top), 0.0)
    inverse = 1.0 / (b - a)
    ab = a * b
    mass = (b * q_left - a * q + ab * (h - h_left)) * inverse
    flux = (b * moment_left - a * moment + ab * (q - q_left)) * inverse
    mass = jnp.where(opened, mass, 0.0)
    left_side = jnp.where(opened, flux, still_left)
    right_side = jnp.where(opened, flux, still)
    h_new = h - step_dt * (rolled(mass, -1) - mass) + step_dt * inflow
    q_new = q - step_dt * (rolled(left_side, -1) - right_side)
    return h_new, q_new


def split(x):
    high = x.astype(jnp.bfloat16)
    return high, (x - high.astype(jnp.float32)).astype(jnp.bfloat16)


def dot(x, y):
    return jnp.dot(x, y, preferred_element_type=jnp.float32)


def dot_t(x, y):
    return lax.dot_general(x, y, (((1,), (1,)), ((), ())), preferred_element_type=jnp.float32)


def kernel(
    quarters, slabs,
    depth, flow, gate, pump, rate, obs_index, obs_value, obs_error,
    out_depth, out_flow,
    d_pad, f_pad, g_pad, p_pad, r_pad, fc_d, fc_f, win_d, win_f, an_d, an_f,
    obs_rows, blocks, edge_src, stats, mem_stats, cell_src, cell_stats, mixing,
    load_sem, halo_send, halo_recv, go_send, go_recv, own_sem,
    edge_send, edge_recv, ms_send, ms_recv, cs_send, cs_recv, back_send, back_recv, back_own,
):
    me = lax.axis_index("mem")
    slab = lax.axis_index("cell")
    rows, cells = depth.shape
    members = rows * quarters
    quart = cells // quarters
    subs = quart // PER
    steps = pump.shape[0]
    total_obs = obs_index.shape[1] * slabs
    pads = (d_pad, f_pad, g_pad, p_pad, r_pad)
    sources = (depth, flow, gate, pump, rate)
    place = slab * quarters + me
    last_place = slabs * quarters - 1
    has_low = slab > 0
    has_high = slab < slabs - 1

    loads = [
        pltpu.make_async_copy(src, pad.at[:, pl.ds(LANES, cells)], load_sem.at[i])
        for i, (src, pad) in enumerate(zip(sources, pads))
    ]
    for copy in loads:
        copy.start()

    barrier = pltpu.get_barrier_semaphore()
    for k in range(1, quarters):
        pl.semaphore_signal(
            barrier, inc=1, device_id={"mem": (me + k) % quarters}, device_id_type=MESH
        )

    def greet(k, _):
        pl.semaphore_signal(barrier, inc=1, device_id={"cell": (slab + k) % slabs}, device_id_type=MESH)
        return 0

    for k in range(1, slabs):
        greet(k, 0)
    cross_low = jnp.logical_and(me == 0, has_low)
    cross_high = jnp.logical_and(me == quarters - 1, has_high)

    @pl.when(cross_low)
    def _():
        pl.semaphore_signal(
            barrier, inc=1, device_id={"mem": quarters - 1, "cell": (slab + slabs - 1) % slabs}, device_id_type=MESH
        )

    @pl.when(cross_high)
    def _():
        pl.semaphore_signal(
            barrier, inc=1, device_id={"mem": 0, "cell": (slab + 1) % slabs}, device_id_type=MESH
        )

    crossing = cross_low.astype(jnp.int32) + cross_high.astype(jnp.int32)
    pl.semaphore_wait(barrier, quarters - 1 + slabs - 1 + crossing)

    def halo(side, i):
        start = cells - LANES if side == 0 else 0
        target = 0 if side == 0 else cells + LANES
        return pltpu.make_async_remote_copy(
            src_ref=sources[i].at[:, pl.ds(start, LANES)],
            dst_ref=pads[i].at[:, pl.ds(target, LANES)],
            send_sem=halo_send.at[side, i],
            recv_sem=halo_recv.at[side, i],
            device_id={"cell": (slab + 1 if side == 0 else slab + slabs - 1) % slabs},
            device_id_type=MESH,
        )

    @pl.when(has_high)
    def _():
        for i in range(5):
            halo(0, i).start()

    @pl.when(has_low)
    def _():
        for i in range(5):
            halo(1, i).start()

    offsets = obs_index[...] - me * quart
    value = obs_value[...]
    precision = 1.0 / obs_error[...]
    coarse = offsets // LANES
    fine = offsets - coarse * LANES
    count = obs_index.shape[1]
    row_count = quart // LANES
    at_row = lax.broadcasted_iota(jnp.int32, (row_count, count), 0) == coarse
    at_lane = (lax.broadcasted_iota(jnp.int32, (LANES, count), 0) == fine).astype(jnp.float32)
    picked = jnp.concatenate(
        [jnp.where(at_row, value, 0.0), jnp.where(at_row, precision, 0.0)], axis=0
    )
    obs_rows[...] = lax.dot_general(
        picked, at_lane, (((1,), (1,)), ((), ())),
        precision=lax.Precision.HIGHEST, preferred_element_type=jnp.float32,
    )

    for copy in loads:
        copy.wait()

    @pl.when(has_low)
    def _():
        for i in range(5):
            halo(0, i).wait_recv()

    @pl.when(has_high)
    def _():
        for i in range(5):
            halo(1, i).wait_recv()

    width = CHUNK + 2 * LANES

    def forecast(chunk):
        start = pl.multiple_of(chunk * CHUNK, CHUNK)
        at = pl.ds(start, width)
        cell = lax.broadcasted_iota(jnp.int32, (1, width), 1) + (slab * cells + start - LANES)
        inside = jnp.logical_and(cell > 0, cell < slabs * cells)
        opened = jnp.logical_and(g_pad[:, at] > 0, inside)
        h = d_pad[:, at]
        q = f_pad[:, at]
        for step in range(steps):
            inflow = r_pad[:, at] * p_pad[step : step + 1, at].astype(jnp.float32)
            h, q = advance(h, q, opened, inflow)
        fc_d[:, pl.ds(start, CHUNK)] = h[:, LANES : LANES + CHUNK]
        fc_f[:, pl.ds(start, CHUNK)] = q[:, LANES : LANES + CHUNK]

    per_quart = quart // CHUNK

    def go(field, k, arriving=False):
        peer = (me + k) % quarters
        owner = (me - k + quarters) % quarters if arriving else me
        source = (fc_d, fc_f)[field]
        target = (win_d, win_f)[field]
        return pltpu.make_async_remote_copy(
            src_ref=source.at[:, pl.ds(pl.multiple_of(peer * quart, quart), quart)],
            dst_ref=target.at[pl.ds(pl.multiple_of(owner * rows, rows), rows), :],
            send_sem=go_send.at[field, k],
            recv_sem=go_recv.at[field, k],
            device_id={"mem": peer},
            device_id_type=MESH,
        )

    def keep(field):
        source = (fc_d, fc_f)[field]
        target = (win_d, win_f)[field]
        return pltpu.make_async_copy(
            source.at[:, pl.ds(pl.multiple_of(me * quart, quart), quart)],
            target.at[pl.ds(pl.multiple_of(me * rows, rows), rows), :],
            own_sem.at[field],
        )

    for k in range(1, quarters + 1):
        peer = (me + k) % quarters

        def one(j, _):
            forecast(peer * per_quart + j)
            return 0

        lax.fori_loop(0, per_quart, one, 0)
        if k < quarters:
            go(0, k).start()
        else:
            keep(0).start()
            keep(1).start()
    for k in range(1, quarters):
        go(1, k).start()

    keep(0).wait()
    keep(1).wait()
    for k in range(1, quarters):
        go(0, k, True).wait_recv()

    pieces = PER // LANES
    extra = 8
    first_extra = lax.broadcasted_iota(jnp.int32, (extra, PER), 0) == 0

    def obs_of(sub, base):
        first_row = base + sub * pieces
        at = [obs_rows[first_row + i : first_row + i + 1, :] for i in range(pieces)]
        return jnp.concatenate(at, axis=1)

    def gram(sub, total):
        x = win_d[:, sub * PER : (sub + 1) * PER]
        mean = jnp.mean(x, axis=0, keepdims=True)
        weight = obs_of(sub, row_count)
        scaled = (x - mean) * weight
        innov = (obs_of(sub, 0) - mean) * weight
        tall = jnp.concatenate(
            [
                scaled,
                jnp.where(first_extra, innov, 0.0),
                jnp.zeros((LANES - members - extra, PER), jnp.float32),
            ],
            axis=0,
        )
        high, low = split(tall)
        part = members + extra
        both = jnp.concatenate([high[:80], low[:80]], axis=0)
        first = dot_t(both, high)
        block = first[:part] + first[80 : 80 + part] + dot_t(high[:80], low)[:part]
        blocks[sub + 1] = block
        return total + block

    part = members + extra
    summed = jnp.zeros((part, LANES), jnp.float32)
    for sub in range(subs):
        summed = gram(sub, summed)
    ri = lax.broadcasted_iota(jnp.int32, (part, LANES), 0)
    ci = lax.broadcasted_iota(jnp.int32, (part, LANES), 1)
    diagonal = jnp.where(ri == ci, summed, 0.0)
    spread = jnp.sum(jnp.where(ri < members, diagonal, 0.0), keepdims=True)
    misfit = jnp.sum(jnp.where(ri == members, diagonal, 0.0), keepdims=True)
    lane = lax.broadcasted_iota(jnp.int32, (8, LANES), 1)
    mine = jnp.where(lane == 0, misfit, jnp.where(lane == 1, spread, 0.0))
    stats[...] = mine
    edge_src[0] = blocks[1]
    edge_src[1] = blocks[subs]

    def tell_mem(k):
        return pltpu.make_async_remote_copy(
            src_ref=stats, dst_ref=mem_stats.at[k],
            send_sem=ms_send.at[k], recv_sem=ms_recv.at[k],
            device_id={"mem": (me + k) % quarters}, device_id_type=MESH,
        )

    for k in range(1, quarters):
        tell_mem(k).start()

    def edge(side):
        other = (place + last_place if side == 0 else place + 1) % (last_place + 1)
        return pltpu.make_async_remote_copy(
            src_ref=edge_src.at[side],
            dst_ref=blocks.at[subs + 1 if side == 0 else 0],
            send_sem=edge_send.at[side], recv_sem=edge_recv.at[side],
            device_id={"mem": other % quarters, "cell": other // quarters},
            device_id_type=MESH,
        )

    @pl.when(place > 0)
    def _():
        edge(0).start()

    @pl.when(place < last_place)
    def _():
        edge(1).start()

    @pl.when(place == 0)
    def _():
        blocks[0] = jnp.zeros((part, LANES), jnp.float32)

    @pl.when(place == last_place)
    def _():
        blocks[subs + 1] = jnp.zeros((part, LANES), jnp.float32)

    for k in range(1, quarters):
        tell_mem(k).wait_recv()
        mine = mine + mem_stats[k]
    cell_src[...] = mine

    def tell_cell(k):
        return pltpu.make_async_remote_copy(
            src_ref=cell_src, dst_ref=cell_stats.at[k],
            send_sem=cs_send.at[k], recv_sem=cs_recv.at[k],
            device_id={"cell": (slab + k) % slabs}, device_id_type=MESH,
        )

    def start_cell(k, _):
        tell_cell(k).start()
        return 0

    for k in range(1, slabs):
        start_cell(k, 0)

    @pl.when(place > 0)
    def _():
        edge(1).wait_recv()

    @pl.when(place < last_place)
    def _():
        edge(0).wait_recv()

    def take_cell(k, total):
        tell_cell(k).wait_recv()
        return total + cell_stats[k]

    total = mine
    for k in range(1, slabs):
        total = take_cell(k, total)
    total = total[:1]
    lane1 = lane[:1]
    misfit = jnp.sum(jnp.where(lane1 == 0, total, 0.0), keepdims=True)
    spread = jnp.sum(jnp.where(lane1 == 1, total, 0.0), keepdims=True)
    rho = jnp.sqrt(misfit / (spread / (members - 1) + total_obs))

    wide = GROUP * members
    wr = lax.broadcasted_iota(jnp.int32, (members, wide), 0)
    wc = lax.broadcasted_iota(jnp.int32, (members, wide), 1)
    eye = jnp.where(wc % members == wr, 1.0, 0.0)
    owner_lane = wc[:1] // members
    sr = lax.broadcasted_iota(jnp.int32, (wide, wide), 0) // members
    sc = lax.broadcasted_iota(jnp.int32, (wide, wide), 1) // members
    own_block = jnp.where(sr == sc, 1.0, 0.0).astype(jnp.bfloat16)

    def spreadout(x):
        return jnp.concatenate([x] * GROUP, axis=0) * own_block

    def times(left, right):
        rh, rl = split(right)
        rh, rl = spreadout(rh), spreadout(rl)
        lh, ll = split(left)
        return dot(lh, rh) + (dot(ll, rh) + dot(lh, rl))

    groups = subs // GROUP
    state = []
    sides = []
    for g in range(groups):
        parts = []
        for p in range(g * GROUP, (g + 1) * GROUP):
            parts.append((blocks[p] + blocks[p + 1] + blocks[p + 2])[:, :members])
        joined = jnp.concatenate(parts, axis=1)
        system = eye + (rho * rho / (members - 1)) * joined[:members]
        squares = jnp.sum(system * system, axis=0, keepdims=True)
        norm = jnp.zeros((1, wide), jnp.float32)
        for p in range(GROUP):
            here = owner_lane == p
            norm = jnp.where(here, jnp.sum(jnp.where(here, squares, 0.0), keepdims=True), norm)
        norm = jnp.sqrt(norm)
        state.append((system / norm, eye))
        sides.append((norm, joined[members:]))

    def newton(_, carry):
        out = []
        for current, invroot in carry:
            factor = 1.5 * eye - 0.5 * times(invroot, current)
            both = times(jnp.concatenate([current, invroot], axis=0), factor)
            out.append((both[:members], both[members:]))
        return tuple(out)

    state = lax.fori_loop(0, NS_ITERS, newton, tuple(state))
    for g in range(groups):
        inverse = state[g][1]
        norm, cross = sides[g]
        solved = times(times(cross, inverse), inverse)[:1] / norm
        mean_weight = rho / (members - 1) * solved
        full = rho * (inverse / jnp.sqrt(norm) + mean_weight)
        high, low = split(full)
        for p in range(GROUP):
            at = slice(p * members, (p + 1) * members)
            mixing[g * GROUP + p] = jnp.concatenate([high[:, at], high[:, at], low[:, at]], axis=1)

    def back(field, sub, k, arriving=False):
        peer = (me + k) % quarters
        owner = (me - k + quarters) % quarters if arriving else me
        source = (an_d, an_f)[field]
        target = (out_depth, out_flow)[field]
        at = pl.multiple_of(sub * PER, PER)
        src_ref = source.at[pl.ds(pl.multiple_of(peer * rows, rows), rows), pl.ds(at, PER)]
        dst_ref = target.at[:, pl.ds(pl.multiple_of(owner * quart + at, PER), PER)]
        return pltpu.make_async_remote_copy(
            src_ref=src_ref, dst_ref=dst_ref,
            send_sem=back_send.at[field, k, sub], recv_sem=back_recv.at[field, k, sub],
            device_id={"mem": peer}, device_id_type=MESH,
        )

    def back_keep(field):
        source = (an_d, an_f)[field]
        target = (out_depth, out_flow)[field]
        return pltpu.make_async_copy(
            source.at[pl.ds(pl.multiple_of(me * rows, rows), rows), :],
            target.at[:, pl.ds(pl.multiple_of(me * quart, quart), quart)],
            back_own.at[field],
        )

    for field in range(2):
        window = (win_d, win_f)[field]
        analysed = (an_d, an_f)[field]
        if field == 1:
            for k in range(1, quarters):
                go(1, k, True).wait_recv()

        def analyse(sub, _):
            at = pl.ds(pl.multiple_of(sub * PER, PER), PER)
            x = window[:, at]
            mean = jnp.mean(x, axis=0, keepdims=True)
            high, low = split(x - mean)
            stacked = jnp.concatenate([high, low, high], axis=0)
            analysed[:, at] = mean + dot(mixing[sub], stacked)
            for k in range(1, quarters):
                back(field, sub, k).start()
            return 0

        for sub in range(subs):
            analyse(sub, 0)
        back_keep(field).start()

    @pl.when(has_high)
    def _():
        for i in range(5):
            halo(0, i).wait_send()

    @pl.when(has_low)
    def _():
        for i in range(5):
            halo(1, i).wait_send()

    @pl.when(place > 0)
    def _():
        edge(0).wait_send()

    @pl.when(place < last_place)
    def _():
        edge(1).wait_send()

    for k in range(1, quarters):
        tell_mem(k).wait_send()
        for field in range(2):
            go(field, k).wait_send()

    def end_cell(k, _):
        tell_cell(k).wait_send()
        return 0

    for k in range(1, slabs):
        end_cell(k, 0)
    for field in range(2):
        back_keep(field).wait()

        def finish(sub, _):
            for k in range(1, quarters):
                back(field, sub, k).wait_send()
                back(field, sub, k, True).wait_recv()
            return 0

        for sub in range(subs):
            finish(sub, 0)


def shards(depth, discharge, gate, pump, pump_rate, obs_index, obs_value, obs_error):
    rows, cells = depth.shape
    slabs = lax.axis_size("cell")
    quarters = lax.axis_size("mem")
    members = rows * quarters
    quart = cells // quarters
    subs = quart // PER
    steps = pump.shape[0]
    padded = cells + 2 * LANES
    part = members + 8
    f32, i32 = jnp.float32, jnp.int32
    dma = pltpu.SemaphoreType.DMA
    scratch = [
        pltpu.VMEM((rows, padded), f32),
        pltpu.VMEM((rows, padded), f32),
        pltpu.VMEM((1, padded), i32),
        pltpu.VMEM((steps, padded), i32),
        pltpu.VMEM((1, padded), f32),
        pltpu.VMEM((rows, cells), f32),
        pltpu.VMEM((rows, cells), f32),
        pltpu.VMEM((members, quart), f32),
        pltpu.VMEM((members, quart), f32),
        pltpu.VMEM((members, quart), f32),
        pltpu.VMEM((members, quart), f32),
        pltpu.VMEM((2 * quart // LANES, LANES), f32),
        pltpu.VMEM((subs + 2, part, LANES), f32),
        pltpu.VMEM((2, part, LANES), f32),
        pltpu.VMEM((8, LANES), f32),
        pltpu.VMEM((quarters, 8, LANES), f32),
        pltpu.VMEM((8, LANES), f32),
        pltpu.VMEM((slabs, 8, LANES), f32),
        pltpu.VMEM((subs, members, 3 * members), jnp.bfloat16),
        dma((5,)),
        dma((2, 5)),
        dma((2, 5)),
        dma((2, quarters)),
        dma((2, quarters)),
        dma((2,)),
        dma((2,)),
        dma((2,)),
        dma((quarters,)),
        dma((quarters,)),
        dma((slabs,)),
        dma((slabs,)),
        dma((2, quarters, subs)),
        dma((2, quarters, subs)),
        dma((2,)),
    ]
    hbm = pl.BlockSpec(memory_space=pl.ANY)
    vmem = pl.BlockSpec(memory_space=pltpu.VMEM)
    return pl.pallas_call(
        functools.partial(kernel, quarters, slabs),
        out_shape=[jax.ShapeDtypeStruct((rows, cells), f32)] * 2,
        in_specs=[hbm] * 5 + [vmem] * 3,
        out_specs=[hbm] * 2,
        scratch_shapes=scratch,
        compiler_params=pltpu.CompilerParams(collective_id=0, has_side_effects=True),
    )(
        depth, discharge, gate.reshape(1, cells), pump, pump_rate.reshape(1, cells),
        obs_index, obs_value, obs_error,
    )


def solution(mesh):
    return jax.shard_map(
        shards,
        mesh=mesh,
        in_specs=(
            P("mem", "cell"),
            P("mem", "cell"),
            P("cell"),
            P(None, "cell"),
            P("cell"),
            P("cell", None),
            P("cell", None),
            P("cell", None),
        ),
        out_specs=(P("mem", "cell"), P("mem", "cell")),
        check_vma=False,
    )
```

time: 182 us -> 81.1 us (0.45)
  Pallas kernels: 0 us -> 76.9 us
  blocking collectives: 58.6 us -> 0 us
  local copies, waits for them, and re-layouts: 49.4 us -> 3.32 us
  matrix products: 26.1 us -> 0 us
  starting transfers between devices: 23.9 us -> 0 us
  other arithmetic: 18 us -> 0 us
  between operations: 3.7 us -> 0.65 us
    pallas_call x0 -> x1, Pallas kernels: none -> 76.9 us  [shards(): pl.pallas_call(functools.partial(kernel, quarters, slabs), out_shape=[jax...]
    all_to_all x1 -> x0, blocking collectives: 29.7 us -> none  [shards(): lax.all_to_all(analysed.reshape(2, members, quart_cells), 'mem', split_ax...]
    dot_general x41 -> x0, matrix products: 26.1 us -> none  [the longest x37 18.8 us: batch_product(): jnp.einsum('uij,ujk->uik', first, second, precision=lax.Precision.HIGHEST)]
    psum x1 -> x0, blocking collectives: 16.1 us -> none  [shards(): lax.psum((jnp.sum(innov_seen * innov_seen), jnp.sum(scaled_seen * scaled_...]
    ppermute x6 -> x0, starting transfers between devices: 15.7 us -> none  [the longest x3 11.9 us: padded_2(): lax.ppermute(lax.slice_in_dim(block, block.shape[dim] - width, None, axis...]
    all_gather x1 -> x0, blocking collectives: 12.8 us -> none  [shards(): seen_all = lax.all_gather(seen_local, 'mem', axis=0, tiled=True)]
    reshape x5 -> x0, local copies, waits for them, and re-layouts: 10 us -> none  [the longest x2 4.03 us: shards(): analysed.reshape(2, members, quart_cells)]
    all_to_all x2 -> x0, starting transfers between devices: 8.12 us -> none  [the longest x1 4.45 us: shards(): lax.all_to_all(flow_quarters, 'mem', split_axis=1, concat_axis=0, tiled=T...]
  transfers between devices with their start and end apart: 8 -> 0, of which waited for: 0 -> 0; matrix products, arithmetic and copies ran while one was open for 20% -> 0% of each run, Pallas kernels for 0% -> 0%
where the time goes in v1:
time: 81.1 us; the launch traced here: 80.9 us
  Pallas kernels  76.9 us (95%)
  local copies, waits for them, and re-layouts  3.32 us (4%)
    pallas_call x1, Pallas kernels, shards(): pl.pallas_call(functools.partial(kernel, quarters, slabs), out_shape=[jax...  76.9 us
    unnamed x4, local copies, waits for them, and re-layouts  3.32 us

profile of v1, /device:TPU:0, one launch (start us, length us, event | category | flops | bytes accessed | tf_op | source)
XLA Modules:
  0.0 80.9 jit_solution(9612983441451137836)
XLA Ops:
  0.6 76.9 %shard_map.95 = (f32[16,16384]{1,0:T(8,128)}, f32[16,16384]{1,0:T(8,128)}) custom-call(f32[16,16384]{1,0:T(8,128)} %depth.1, f32[16,16384]{1,0:T(8,128)} %flow.1, s32[1,16384]{1,0:T(1,128)} %bitcast.2, s32[2,16384]{1,0:T(2,128)} %pump.1, f32[1,16384]{1,0:T(1,128)} %bitcast.3, s32[1,512]{1,0:T(1,128)} %obs_index.1, f32[1,512]{1,0:T(1,128)} %obs_value.1, ...), custom_call_target="tpu_custom_call" | custom-call | tf_op jit(solution)/shard_map/pallas_call | solution.py:553
  77.6 0.0 copy-start
  77.6 2.4 %copy.12 = f32[16,16384]{1,0:T(8,128)} copy(f32[16,16384]{1,0:T(8,128)} %get-tuple-element.4) | data formatting | bytes 2097152
  79.9 0.0 copy-done
  79.9 1.0 %copy.13 = f32[16,16384]{1,0:T(8,128)} copy(f32[16,16384]{1,0:T(8,128)S(1)} %copy-done) | data formatting | bytes 2097152
Async XLA Ops:
  77.6 2.4 %copy-start = (f32[16,16384]{1,0:T(8,128)S(1)}, f32[16,16384]{1,0:T(8,128)}, u32[]{:S(2)}) copy-start(f32[16,16384]{1,0:T(8,128)} %get-tuple-element.5) | copy-start | bytes 3145732

commit v2 on v1

--- a/solution.py
+++ b/solution.py
@@ -10,7 +10,7 @@
 PER = 512
 NS_ITERS = 12
 LANES = 128
-CHUNK = 1024
+CHUNK = 2048
 GROUP = 4
 MESH = pl.DeviceIdType.MESH
 

time: 81.1 us -> 80 us (0.986)
  Pallas kernels: 76.9 us -> 75.8 us
    pallas_call x1, Pallas kernels: 76.9 us -> 75.8 us  [shards(): pl.pallas_call(functools.partial(kernel, quarters, slabs), out_shape=[jax...]
where the time goes in v2:
time: 80 us; the launch traced here: 79.8 us
  Pallas kernels  75.8 us (95%)
  local copies, waits for them, and re-layouts  3.32 us (4%)
    pallas_call x1, Pallas kernels, shards(): pl.pallas_call(functools.partial(kernel, quarters, slabs), out_shape=[jax...  75.8 us
    unnamed x4, local copies, waits for them, and re-layouts  3.32 us

profile of v2, /device:TPU:0, one launch (start us, length us, event | category | flops | bytes accessed | tf_op | source)
XLA Modules:
  0.0 79.8 jit_solution(3935819958969480083)
XLA Ops:
  0.6 75.8 %shard_map.95 = (f32[16,16384]{1,0:T(8,128)}, f32[16,16384]{1,0:T(8,128)}) custom-call(f32[16,16384]{1,0:T(8,128)} %depth.1, f32[16,16384]{1,0:T(8,128)} %flow.1, s32[1,16384]{1,0:T(1,128)} %bitcast.2, s32[2,16384]{1,0:T(2,128)} %pump.1, f32[1,16384]{1,0:T(1,128)} %bitcast.3, s32[1,512]{1,0:T(1,128)} %obs_index.1, f32[1,512]{1,0:T(1,128)} %obs_value.1, ...), custom_call_target="tpu_custom_call" | custom-call | tf_op jit(solution)/shard_map/pallas_call | solution.py:553
  76.5 0.0 copy-start
  76.5 2.4 %copy.12 = f32[16,16384]{1,0:T(8,128)} copy(f32[16,16384]{1,0:T(8,128)} %get-tuple-element.4) | data formatting | bytes 2097152
  78.8 0.0 copy-done
  78.8 1.0 %copy.13 = f32[16,16384]{1,0:T(8,128)} copy(f32[16,16384]{1,0:T(8,128)S(1)} %copy-done) | data formatting | bytes 2097152
Async XLA Ops:
  76.5 2.4 %copy-start = (f32[16,16384]{1,0:T(8,128)S(1)}, f32[16,16384]{1,0:T(8,128)}, u32[]{:S(2)}) copy-start(f32[16,16384]{1,0:T(8,128)} %get-tuple-element.5) | copy-start | bytes 3145732
